TPU v7x, 512 devices: a whole 4x8x8 slice. The times are simulated.
512 devices in a mesh: row: 32 (over y, x), col: 16 (over z, core).
Axes of the slice: x: 4, y: 8, z: 8, core: 2. Of those that a mesh axis runs over, the one named last changes fastest.
Arguments:
- density: bfloat16 [4096, 4096], P('row', 'col'), as said below
- cotangent: bfloat16 [4096, 4096], P('row', 'col'), may hold values from -6 to 6
- block_pattern: int32 [64, 64], P('row', 'col'), may hold values from 0 to 1, as said below
- filter_pattern: int32 [64, 64], P('row', 'col'), may hold values from 0 to 1, as said below
Outputs:
- purified: bfloat16 [4096, 4096], P('row', 'col')
- gradient: bfloat16 [4096, 4096], P('row', 'col')
Inputs may be any that keep to these rules, and one draw needn't show every extreme that they name: density is symmetric. `block_pattern`: symmetric, with ones on the diagonal. `filter_pattern`: symmetric, with ones on the diagonal.
All inputs are finite; a program needn't handle non-finite values.
Results may differ from a plain program's by a relative error of at most 0.0043.
Values may be sent and summed in bfloat16 or wider, within the bound.
A program may use at most 64 MiB of HBM per device.

v0:
```python
import jax
import jax.numpy as jnp
from jax import lax
from jax.sharding import PartitionSpec as P


def expand(pattern, block_size):
    height, width = pattern.shape
    spread = jnp.broadcast_to(pattern[:, None, :, None], (height, block_size, width, block_size))
    return spread.reshape(height * block_size, width * block_size).astype(jnp.float32)


def on_device(density, cotangent, block_pattern, filter_pattern):
    block_size = density.shape[0] // block_pattern.shape[0]
    keep_p = expand(block_pattern, block_size)
    keep_f = expand(filter_pattern, block_size)
    masked = (density.astype(jnp.float32) * keep_p).astype(jnp.bfloat16)
    weighted = (-2.0 * cotangent.astype(jnp.float32) * keep_f).astype(jnp.bfloat16)
    masked_rows, weighted_rows = (
        lax.all_gather(masked, "col", axis=1, tiled=True),
        lax.all_gather(weighted, "col", axis=1, tiled=True),
    )
    masked_cols, weighted_cols = (
        lax.all_gather(masked, "row", axis=0, tiled=True),
        lax.all_gather(weighted, "row", axis=0, tiled=True),
    )
    square = (
        jnp.dot(masked_rows, masked_cols, preferred_element_type=jnp.float32) * keep_f
    ).astype(jnp.bfloat16)
    back_term = jnp.dot(weighted_rows, masked_cols, preferred_element_type=jnp.float32)
    square_rows = lax.all_gather(square, "col", axis=1, tiled=True)
    cubic_term = jnp.dot(square_rows, masked_cols, preferred_element_type=jnp.float32) * keep_f
    purified = (3.0 * square.astype(jnp.float32) - 2.0 * cubic_term).astype(jnp.bfloat16)
    square_grad = ((3.0 * cotangent.astype(jnp.float32) + back_term) * keep_f).astype(jnp.bfloat16)
    grad_rows = lax.all_gather(square_grad, "col", axis=1, tiled=True)
    grad_cols = lax.all_gather(square_grad, "row", axis=0, tiled=True)
    paired = jnp.dot(square_rows, weighted_cols, preferred_element_type=jnp.float32)
    paired = paired + jnp.dot(masked_rows, grad_cols, preferred_element_type=jnp.float32)
    summed = paired + jnp.dot(grad_rows, masked_cols, preferred_element_type=jnp.float32)
    gradient = (summed * keep_p).astype(jnp.bfloat16)
    return (purified, gradient)


def solution(mesh):
    placed = (P("row", "col"), P("row", "col"), P("row", "col"), P("row", "col"))
    return jax.shard_map(
        on_device,
        mesh=mesh,
        in_specs=placed,
        out_specs=(P("row", "col"), P("row", "col")),
        check_vma=False,
    )
```

profile of v0, /device:TPU:1, one launch (start us, length us, event | category | flops | bytes accessed | tf_op | source)
XLA Modules:
  0.0 445.2 jit_solution(4373424468250809988)
XLA Ops:
  7.2 0.7 convert_element_type.43
  7.9 0.1 broadcast_in_dim.4
  8.0 0.2 convert_element_type.44
  8.2 1.5 multiply_convert_fusion
  9.8 0.7 all-gather.10.cloned.1.call-update
  10.5 0.7 convert_element_type.46
  11.2 0.1 broadcast_in_dim.5
  11.3 0.2 convert_element_type.47
  11.5 1.5 fusion.9
  13.1 0.5 all-gather.14.cloned.1.call-update
  13.7 43.7 %all-gather.8.cloned.1.call-done = bf16[128,4096]{1,0:T(8,128)(2,1)} async-done(((bf16[128,256]{1,0:T(8,128)(2,1)}), bf16[128,4096]{1,0:T(8,128)(2,1)}) %all-gather.8.cloned.1.call-update) | async-done | bytes 1048592 | tf_op jit(solution)/shard_map/all_gather | solution.py:20
  57.4 80.7 %all-gather.10.cloned.1.call-done = bf16[4096,256]{1,0:T(8,128)(2,1)} async-done(((bf16[128,256]{1,0:T(8,128)(2,1)}), bf16[4096,256]{1,0:T(8,128)(2,1)}) %all-gather.10.cloned.1.call-update) | async-done | bytes 2097168 | tf_op jit(solution)/shard_map/all_gather | solution.py:24
  138.0 3.1 fusion.4
  141.2 42.9 %all-gather.16.cloned.1.call-done = bf16[128,4096]{1,0:T(8,128)(2,1)} async-done(((bf16[128,256]{1,0:T(8,128)(2,1)}), bf16[128,4096]{1,0:T(8,128)(2,1)}) %all-gather.16.cloned.1.call-update) | async-done | bytes 1048592 | tf_op jit(solution)/shard_map/all_gather | solution.py:21
  184.1 2.3 fusion.6
  186.5 0.7 all-gather.20.cloned.1.call-update
  187.2 77.4 %all-gather.14.cloned.1.call-done = bf16[4096,256]{1,0:T(8,128)(2,1)} async-done(((bf16[128,256]{1,0:T(8,128)(2,1)}), bf16[4096,256]{1,0:T(8,128)(2,1)}) %all-gather.14.cloned.1.call-update) | async-done | bytes 2097168 | tf_op jit(solution)/shard_map/all_gather | solution.py:25
  264.7 45.9 %all-gather.12.cloned.1.call-done = bf16[128,4096]{1,0:T(8,128)(2,1)} async-done(((bf16[128,256]{1,0:T(8,128)(2,1)}), bf16[128,4096]{1,0:T(8,128)(2,1)}) %all-gather.12.cloned.1.call-update) | async-done | bytes 1048592 | tf_op jit(solution)/shard_map/all_gather | solution.py:31
  310.6 3.1 fusion.10
  313.7 1.1 fusion.5
  314.8 75.8 %all-gather.18.cloned.1.call-done = bf16[4096,256]{1,0:T(8,128)(2,1)} async-done(((bf16[128,256]{1,0:T(8,128)(2,1)}), bf16[4096,256]{1,0:T(8,128)(2,1)}) %all-gather.18.cloned.1.call-update) | async-done | bytes 2097168 | tf_op jit(solution)/shard_map/all_gather | solution.py:36
  390.5 2.0 convolution_add_fusion.1
  392.6 43.5 %all-gather.20.cloned.1.call-done = bf16[128,4096]{1,0:T(8,128)(2,1)} async-done(((bf16[128,256]{1,0:T(8,128)(2,1)}), bf16[128,4096]{1,0:T(8,128)(2,1)}) %all-gather.20.cloned.1.call-update) | async-done | bytes 1048592 | tf_op jit(solution)/shard_map/all_gather | solution.py:35
  436.1 2.3 fusion.7
  (21 shorter events, 0.4 us)
Async XLA Ops:
  7.2 50.2 %all-gather.8.cloned.1.call-start = ((), (), s32[]{:S(2)}) async-start(), calls=%async_computation | async-start | bytes 1114112 | tf_op jit(solution)/shard_map/all_gather | solution.py:20
  9.7 128.3 %all-gather.10.cloned.1.call-start = ((), (), s32[]{:S(2)}) async-start(), calls=%async_computation.1 | async-start | bytes 2162688 | tf_op jit(solution)/shard_map/all_gather | solution.py:24
  10.5 173.7 %all-gather.16.cloned.1.call-start = ((), (), s32[]{:S(2)}) async-start(), calls=%async_computation.4 | async-start | bytes 1114112 | tf_op jit(solution)/shard_map/all_gather | solution.py:21
  11.3 172.8 %copy-start.4 = (bf16[128,256]{1,0:T(8,128)(2,1)S(1)}, bf16[128,256]{1,0:T(8,128)(2,1)}, u32[]{:S(2)}) copy-start(bf16[128,256]{1,0:T(8,128)(2,1)} %param.5) | copy-start | bytes 196612
  13.0 251.6 %all-gather.14.cloned.1.call-start = ((), (), s32[]{:S(2)}) async-start(), calls=%async_computation.3 | async-start | bytes 2162688 | tf_op jit(solution)/shard_map/all_gather | solution.py:25
  13.6 297.0 %all-gather.12.cloned.1.call-start = ((), (), s32[]{:S(2)}) async-start(), calls=%async_computation.2 | async-start | bytes 1114112 | tf_op jit(solution)/shard_map/all_gather | solution.py:31
  138.0 46.1 %copy-start = (bf16[4096,256]{1,0:T(8,128)(2,1)S(1)}, bf16[4096,256]{1,0:T(8,128)(2,1)}, u32[]{:S(2)}) copy-start(bf16[4096,256]{1,0:T(8,128)(2,1)} %all-gather.10.cloned.1.call-done) | copy-start | bytes 6291460
  141.2 249.4 %all-gather.18.cloned.1.call-start = ((), (), s32[]{:S(2)}) async-start(), calls=%async_computation.5 | async-start | bytes 2162688 | tf_op jit(solution)/shard_map/all_gather | solution.py:36
  186.4 127.2 %copy-start.3 = (bf16[128,256]{1,0:T(8,128)(2,1)S(1)}, bf16[128,256]{1,0:T(8,128)(2,1)}, u32[]{:S(2)}) copy-start(bf16[128,256]{1,0:T(8,128)(2,1)} %fusion.4) | copy-start | bytes 196612
  186.5 249.6 %all-gather.20.cloned.1.call-start = ((), (), s32[]{:S(2)}) async-start(), calls=%async_computation.6 | async-start | bytes 1114112 | tf_op jit(solution)/shard_map/all_gather | solution.py:35
  310.6 3.1 copy-start.2
  313.7 76.9 %copy-start.1 = (bf16[128,4096]{1,0:T(8,128)(2,1)S(1)}, bf16[128,4096]{1,0:T(8,128)(2,1)}, u32[]{:S(2)}) copy-start(bf16[128,4096]{1,0:T(8,128)(2,1)} %all-gather.8.cloned.1.call-done) | copy-start | bytes 3145732
Sparse Core Ops, SparseCore 0:
  10.6 46.7 all-gather.7
  61.1 76.8 all-gather.9
  140.7 43.4 all-gather.15
  187.7 76.8 all-gather.13
  267.1 43.4 all-gather.11
  313.6 76.8 all-gather.17
  392.6 43.4 all-gather.19
where the time goes:
time: 446 us; the launch traced here: 445 us
  waiting for transfers between devices  412 us (92%)
  between operations  14.2 us (3%)
  matrix products  13.9 us (3%)
    all_gather x1, waiting for transfers between devices, on_device(): lax.all_gather(masked, 'row', axis=0, tiled=True)  80.7 us
    all_gather x1, waiting for transfers between devices, on_device(): lax.all_gather(weighted, 'row', axis=0, tiled=True)  77.4 us
    all_gather x1, waiting for transfers between devices, on_device(): grad_cols = lax.all_gather(square_grad, 'row', axis=0, tiled=True)  75.8 us
    all_gather x1, waiting for transfers between devices, on_device(): square_rows = lax.all_gather(square, 'col', axis=1, tiled=True)  45.9 us
    all_gather x1, waiting for transfers between devices, on_device(): lax.all_gather(masked, 'col', axis=1, tiled=True)  43.7 us
    all_gather x1, waiting for transfers between devices, on_device(): grad_rows = lax.all_gather(square_grad, 'col', axis=1, tiled=True)  43.5 us
    all_gather x1, waiting for transfers between devices, on_device(): lax.all_gather(weighted, 'col', axis=1, tiled=True)  42.9 us
  transfers between devices with their start and end apart: 7, of which 7 were waited for; matrix products, arithmetic and copies ran while one was open for 3% of the time, Pallas kernels for 0%

commit v1 on v0

v1 whole, which is shorter than its diff:
```python
import functools

import jax
import jax.numpy as jnp
from jax import lax
from jax.experimental import pallas as pl
from jax.experimental.pallas import tpu as pltpu
from jax.sharding import PartitionSpec as P

MESH = pl.DeviceIdType.MESH
X = 4
MID_TYPE = jnp.float32
END_TYPE = jnp.bfloat16
N_SEM = 224


class Net:
    def __init__(self, send_sem, recv_sem):
        self.send_sem, self.recv_sem, self.used, self.sent = send_sem, recv_sem, 0, []

    def take(self, count):
        first = self.used
        self.used += count
        assert self.used <= N_SEM
        return first

    def send(self, src, dst, sem, recv, device):
        copy = pltpu.make_async_remote_copy(
            src_ref=src,
            dst_ref=dst,
            send_sem=self.send_sem.at[sem],
            recv_sem=self.recv_sem.at[recv],
            device_id=device,
            device_id_type=MESH,
        )
        copy.start()
        self.sent.append((copy, None))

    def send_or_keep(self, src, dst, sem, recv, device, is_self):
        copy = pltpu.make_async_remote_copy(
            src_ref=src,
            dst_ref=dst,
            send_sem=self.send_sem.at[sem],
            recv_sem=self.recv_sem.at[recv],
            device_id=device,
            device_id_type=MESH,
        )

        @pl.when(is_self)
        def _():
            pltpu.make_async_copy(src, dst, self.recv_sem.at[recv]).start()

        @pl.when(jnp.logical_not(is_self))
        def _():
            copy.start()

        self.sent.append((copy, is_self))

    def wait(self, dst, recv):
        pltpu.make_async_copy(dst, dst, self.recv_sem.at[recv]).wait()

    def drain(self):
        for copy, is_self in self.sent:
            if is_self is None:
                copy.wait_send()
            else:

                @pl.when(jnp.logical_not(is_self))
                def _():
                    copy.wait_send()


class Ring:
    def __init__(self, net, view, me, n, plus, minus, partner=None, other=None, long_plus=True):
        self.net, self.view, self.me, self.n = net, view, me, n
        self.plus, self.minus, self.partner, self.other = plus, minus, partner, other
        half, rest = n // 2, n - 1 - n // 2
        self.hops = (half, rest) if long_plus else (rest, half)
        self.up, self.down = net.take(self.hops[0]), net.take(self.hops[1])
        if partner is not None:
            self.cross = net.take(n)

    def block(self, hop, sign):
        return lax.rem(self.me + self.n - sign * hop, self.n)

    def start(self):
        mine = self.view(self.me)
        if self.hops[0]:
            self.net.send(mine, mine, self.up, self.up, self.plus)
        if self.hops[1]:
            self.net.send(mine, mine, self.down, self.down, self.minus)
        if self.partner is not None:
            self.net.send(mine, mine, self.cross, self.cross, self.partner)

    def step(self, s):
        for way, sign, first, to in ((0, 1, self.up, self.plus), (1, -1, self.down, self.minus)):
            if s < self.hops[way]:
                got = self.view(self.block(s + 1, sign))
                self.net.wait(got, first + s)
                if s + 1 < self.hops[way]:
                    self.net.send(got, got, first + s + 1, first + s + 1, to)
                if self.partner is not None:
                    at = self.cross + 1 + s + way * self.hops[0]
                    self.net.send(got, got, at, at, self.partner)

    def steps(self):
        return max(self.hops)

    def finish_cross(self):
        self.net.wait(self.other(self.me), self.cross)
        for way, sign in ((0, 1), (1, -1)):
            for s in range(self.hops[way]):
                at = self.cross + 1 + s + way * self.hops[0]
                self.net.wait(self.other(self.block(s + 1, sign)), at)


def spread(pattern, rows):
    lane = lax.broadcasted_iota(jnp.int32, (rows // 2, 256), 1)
    halves = []
    for i in range(2):
        e = [pattern[i, j].astype(jnp.float32) for j in range(4)]
        low = jnp.where(lane < 64, e[0], e[1])
        high = jnp.where(lane < 192, e[2], e[3])
        halves.append(jnp.where(lane < 128, low, high))
    return jnp.concatenate(halves, axis=0)


def kernel(
    ny, nz, den_ref, cot_ref, pat_ref, fil_ref, pur_ref, grad_ref,
    am, aw, asq, ag, bm, bw, bg, keep_mine, keep_tile, part_s, part_g, got_s, got_g, square_end,
    end_p, end_g, got_p, got_d, send_sem, recv_sem,
):
    row, col = lax.axis_index("row"), lax.axis_index("col")
    x, y = lax.rem(row, X), lax.div(row, X)
    core, z = lax.rem(col, 2), lax.div(col, 2)

    def dev(yy, xx, zz, cc):
        return (yy * X + xx, zz * 2 + cc)

    partner = dev(y, x, z, 1 - core)
    y_up, y_down = dev(lax.rem(y + 1, ny), x, z, core), dev(lax.rem(y + ny - 1, ny), x, z, core)
    z_up, z_down = dev(y, x, lax.rem(z + 1, nz), core), dev(y, x, lax.rem(z + nz - 1, nz), core)
    others = [partner, y_up, y_down, z_up, z_down]
    for d in range(1, X):
        there = lax.rem(x + d, X)
        others += [dev(y, there, z, core), dev(y, there, z, 1 - core)]

    barrier = pltpu.get_barrier_semaphore()
    for other in others:
        pl.semaphore_signal(barrier, inc=1, device_id=other, device_id_type=MESH)
    keep_p = spread(pat_ref, 128)
    keep_f = spread(fil_ref, 128)
    bm[y, core] = (den_ref[...].astype(jnp.float32) * keep_p).astype(jnp.bfloat16)
    bw[y, core] = (-2.0 * cot_ref[...].astype(jnp.float32) * keep_f).astype(jnp.bfloat16)
    keep_mine[...] = keep_f.astype(jnp.bfloat16)
    pl.semaphore_wait(barrier, len(others))

    net = Net(send_sem, recv_sem)
    slot = lax.rem(x, 2)
    home = lax.div(x, 2)

    def swap(src, dst):
        send, recv = net.take(2), net.take(2)
        for j in range(2):
            is_self = jnp.logical_and(x == 2 * core + j, home == core)
            net.send_or_keep(src(j), dst(slot), send + j, recv + slot, dev(y, 2 * core + j, z, home), is_self)
        return recv

    def to_rows(own, tile):
        return (lambda j: own.at[:, pl.ds(128 * j, 128)]), (lambda s: tile.at[pl.ds(pl.multiple_of(128 * s, 128), 128), :])

    def to_cols(tile, own):
        return (lambda j: tile.at[pl.ds(128 * j, 128), :]), (lambda s: own.at[:, pl.ds(pl.multiple_of(128 * s, 128), 128)])

    def wait_swap(dst, recv):
        for s in range(2):
            net.wait(dst(s), recv + s)

    def b_ring(buf, long_plus):
        return Ring(net, lambda k: buf.at[k, core], y, ny, y_up, y_down, partner, lambda k: buf.at[k, 1 - core], long_plus)

    def a_ring(buf, long_plus):
        return Ring(net, lambda k: buf.at[k], z, nz, z_up, z_down, None, None, long_plus)

    def product(a, b, h):
        left = jnp.concatenate([a[k] for k in range(nz)], axis=1)
        right = b[:, h].reshape(ny * 128, 256)
        return jnp.dot(left, right, preferred_element_type=jnp.float32)

    def part(a, b, to):
        for h in range(2):
            value = product(a, b, h)
            to[2 * h] = value[:, :128]
            to[2 * h + 1] = value[:, 128:]

    def reduce_start(src, dst):
        sems = net.take(X)
        for d in range(1, X):
            there = lax.rem(x + d, X)
            net.send(src.at[there], dst.at[d], sems + d, sems + d, dev(y, there, z, core))
        return sems

    def reduce_end(src, dst, sems):
        total = src[x]
        for d in range(1, X):
            net.wait(dst.at[d], sems + d)
            total = total + dst[d].astype(jnp.float32)
        return total

    def end_start(src, dst):
        send, recv = net.take(4), net.take(X)
        for j in range(2):
            for h in range(2):
                is_self = jnp.logical_and(x == 2 * core + j, core == h)
                net.send_or_keep(src.at[j, h], dst.at[x], send + 2 * j + h, recv + x, dev(y, 2 * core + j, z, h), is_self)
        return recv

    def end_sum(dst, recv):
        total = None
        for s in range(X):
            net.wait(dst.at[s], recv + s)
            term = dst[s].astype(jnp.float32)
            total = term if total is None else total + term
        return total

    w_src, w_dst = to_rows(bw.at[y, core], aw.at[z])
    m_src, m_dst = to_rows(bm.at[y, core], am.at[z])
    f_src, f_dst = to_rows(keep_mine, keep_tile)
    w_swap = swap(w_src, w_dst)
    m_swap = swap(m_src, m_dst)
    ring_bm = b_ring(bm, True)
    ring_bm.start()
    f_swap = swap(f_src, f_dst)
    ring_aw, ring_am = a_ring(aw, True), a_ring(am, False)
    wait_swap(w_dst, w_swap)
    ring_aw.start()
    wait_swap(m_dst, m_swap)
    ring_am.start()
    for s in range(ring_bm.steps()):
        ring_bm.step(s)
        ring_aw.step(s)
        ring_am.step(s)
    ring_bm.finish_cross()

    part(aw, bm, part_g)
    g_sems = reduce_start(part_g, got_g)
    part(am, bm, part_s)
    s_sems = reduce_start(part_s, got_s)
    ring_bw = b_ring(bw, False)
    ring_bw.start()
    wait_swap(f_dst, f_swap)

    grad = -1.5 * aw[z].astype(jnp.float32) + reduce_end(part_g, got_g, g_sems)
    ag[z] = (grad * keep_tile[...].astype(jnp.float32)).astype(jnp.bfloat16)
    ring_ag = a_ring(ag, True)
    ring_ag.start()
    g_src, g_dst = to_cols(ag.at[z], bg.at[y, core])
    g_swap = swap(g_src, lambda s: bg.at[y, home, :, pl.ds(pl.multiple_of(128 * s, 128), 128)])

    asq[z] = (reduce_end(part_s, got_s, s_sems) * keep_tile[...].astype(jnp.float32)).astype(jnp.bfloat16)
    ring_as = a_ring(asq, False)
    ring_as.start()
    wait_swap(g_dst, g_swap)
    ring_bg = b_ring(bg, True)
    ring_bg.start()
    q_src, q_dst = to_cols(asq.at[z], square_end)
    q_swap = swap(q_src, q_dst)
    for s in range(ring_bw.steps()):
        ring_bw.step(s)
        ring_ag.step(s)
        ring_as.step(s)
        ring_bg.step(s)
    ring_bw.finish_cross()

    for h in range(2):
        value = product(asq, bm, h).astype(END_TYPE)
        for j in range(2):
            end_p[j, h] = value[128 * j : 128 * j + 128]
    p_recv = end_start(end_p, got_p)
    ring_bg.finish_cross()
    for h in range(2):
        value = (product(asq, bw, h) + product(ag, bm, h) + product(am, bg, h)).astype(END_TYPE)
        for j in range(2):
            end_g[j, h] = value[128 * j : 128 * j + 128]
    d_recv = end_start(end_g, got_d)

    wait_swap(q_dst, q_swap)
    cubic = end_sum(got_p, p_recv) * keep_mine[...].astype(jnp.float32)
    pur_ref[...] = (3.0 * square_end[...].astype(jnp.float32) - 2.0 * cubic).astype(jnp.bfloat16)
    grad_ref[...] = (end_sum(got_d, d_recv) * spread(pat_ref, 128)).astype(jnp.bfloat16)
    net.drain()


def on_device(ny, nz, density, cotangent, block_pattern, filter_pattern):
    bf16, f32 = jnp.bfloat16, jnp.float32
    left = pltpu.VMEM((nz, 256, 128), bf16)
    right = pltpu.VMEM((ny, 2, 128, 256), bf16)
    block = pltpu.VMEM((128, 256), bf16)
    vmem = pl.BlockSpec(memory_space=pltpu.VMEM)
    smem = pl.BlockSpec(memory_space=pltpu.SMEM)
    return pl.pallas_call(
        functools.partial(kernel, ny, nz),
        out_shape=(jax.ShapeDtypeStruct((128, 256), bf16),) * 2,
        in_specs=[vmem, vmem, smem, smem],
        out_specs=(vmem, vmem),
        scratch_shapes=[left] * 4
        + [right] * 3
        + [
            block,
            pltpu.VMEM((256, 128), bf16),
            pltpu.VMEM((X, 256, 128), f32),
            pltpu.VMEM((X, 256, 128), f32),
            pltpu.VMEM((X, 256, 128), MID_TYPE),
            pltpu.VMEM((X, 256, 128), MID_TYPE),
            block,
            pltpu.VMEM((2, 2, 128, 256), END_TYPE),
            pltpu.VMEM((2, 2, 128, 256), END_TYPE),
            pltpu.VMEM((X, 128, 256), END_TYPE),
            pltpu.VMEM((X, 128, 256), END_TYPE),
            pltpu.SemaphoreType.DMA((N_SEM,)),
            pltpu.SemaphoreType.DMA((N_SEM,)),
        ],
        compiler_params=pltpu.CompilerParams(collective_id=0, has_side_effects=True),
    )(density, cotangent, block_pattern, filter_pattern)


def solution(mesh):
    ny, nz = mesh.shape["row"] // X, mesh.shape["col"] // 2
    placed = (P("row", "col"),) * 4
    return jax.shard_map(
        functools.partial(on_device, ny, nz),
        mesh=mesh,
        in_specs=placed,
        out_specs=(P("row", "col"), P("row", "col")),
        check_vma=False,
    )
```

time: 446 us -> 80.2 us (0.18)
  waiting for transfers between devices: 412 us -> 0 us
  Pallas kernels: 0 us -> 77.2 us
  matrix products: 13.9 us -> 0 us
  between operations: 14.2 us -> 0.65 us
    all_gather x7 -> x0, waiting for transfers between devices: 410 us -> none  [the longest x1 80.7 us: on_device(): lax.all_gather(masked, 'row', axis=0, tiled=True)]
    pallas_call x0 -> x1, Pallas kernels: none -> 77.2 us  [on_device(): pl.pallas_call(functools.partial(kernel, ny, nz), out_shape=(jax.ShapeDty...]
    dot_general x6 -> x0, matrix products: 13.9 us -> none  [the longest x1 3.13 us: on_device(): jnp.dot(masked_rows, masked_cols, preferred_element_type=jnp.float32)]
  transfers between devices with their start and end apart: 7 -> 0, of which waited for: 7 -> 0; matrix products, arithmetic and copies ran while one was open for 3% -> 0% of each run, Pallas kernels for 0% -> 0%
where the time goes in v1:
time: 80.2 us; the launch traced here: 80 us
  Pallas kernels  77.2 us (96%)
  local copies, waits for them, and re-layouts  2.14 us (3%)
    pallas_call x1, Pallas kernels, on_device(): pl.pallas_call(functools.partial(kernel, ny, nz), out_shape=(jax.ShapeDty...  77.2 us
    unnamed x4, local copies, waits for them, and re-layouts  2.14 us

profile of v1, /device:TPU:1, one launch (start us, length us, event | category | flops | bytes accessed | tf_op | source)
XLA Modules:
  0.0 80.0 jit_solution(1695434474014772991)
XLA Ops:
  0.6 77.2 %shard_map.59 = (bf16[128,256]{1,0:T(8,128)(2,1)}, bf16[128,256]{1,0:T(8,128)(2,1)}) custom-call(bf16[128,256]{1,0:T(8,128)(2,1)} %den_ref.1, bf16[128,256]{1,0:T(8,128)(2,1)} %cot_ref.1, s32[2,4]{1,0:T(2,128)} %pat_ref.1, s32[2,4]{1,0:T(2,128)} %fil_ref.1), custom_call_target="tpu_custom_call" | custom-call | tf_op jit(solution)/shard_map/pallas_call | solution.py:301
  77.9 0.0 copy-start
  77.9 1.5 %copy.8 = bf16[128,256]{1,0:T(8,128)(2,1)} copy(bf16[128,256]{1,0:T(8,128)(2,1)} %get-tuple-element.4) | data formatting | bytes 131072
  79.4 0.0 copy-done
  79.4 0.6 copy.9
Async XLA Ops:
  77.9 1.5 %copy-start = (bf16[128,256]{1,0:T(8,128)(2,1)S(1)}, bf16[128,256]{1,0:T(8,128)(2,1)}, u32[]{:S(2)}) copy-start(bf16[128,256]{1,0:T(8,128)(2,1)} %get-tuple-element.5) | copy-start | bytes 196612

commit v2 on v1

v2 whole, which is shorter than its diff:
```python
import functools

import jax
import jax.numpy as jnp
from jax import lax
from jax.experimental import pallas as pl
from jax.experimental.pallas import tpu as pltpu
from jax.sharding import PartitionSpec as P

MESH = pl.DeviceIdType.MESH
X = 4
MID_TYPE = jnp.bfloat16
END_TYPE = jnp.bfloat16
N_SEM = 100
PLAN = dict(bm="two", aw="two", am="two", bw="two", ag="two", asq="two", bg="two")
PLANS = {
    "ring": (((0, None, 1), (0, None, -1)), ((-1, None, 1), (1, None, -1)), ((-2, None, 1), (2, None, -1)), ((-3, 0, 1), (3, 1, -1))),
    "two": (((0, None, 2), (0, None, -2), (0, None, 1), (0, None, -1)), ((-2, None, 1), (2, None, -1), (-2, 0, 2), (2, 1, -2))),
}
FAR = 2


class Net:
    def __init__(self, sems, ruler, at_home):
        self.sems, self.ruler, self.at_home, self.used, self.later = sems, ruler, at_home, 0, []

    def take(self):
        self.used += 1
        assert self.used <= N_SEM
        return self.used - 1

    def copy(self, src, dst, send, recv, device):
        return pltpu.make_async_remote_copy(
            src_ref=src,
            dst_ref=dst,
            send_sem=self.sems.at[send],
            recv_sem=self.sems.at[recv],
            device_id=device,
            device_id_type=MESH,
        )

    def send(self, src, dst, send, recv, device):
        self.copy(src, dst, send, recv, device).start()

    def send_or_keep(self, src, dst, send, recv, device, is_self):
        @pl.when(is_self)
        def _():
            pltpu.make_async_copy(src, dst, self.sems.at[recv]).start()

        @pl.when(jnp.logical_not(is_self))
        def _():
            self.copy(src, dst, send, recv, device).start()

    def wait(self, dst, sem):
        pltpu.make_async_copy(dst, dst, self.sems.at[sem]).wait()

    def sent(self, sem, units, home_units=None):
        self.later.append((sem, units, home_units))

    def wait_units(self, sem, units):
        view = self.ruler.at[0, pl.ds(0, 128)] if units == 1 else self.ruler.at[pl.ds(0, units // 2)]
        self.wait(view, sem)

    def drain(self):
        for sem, units, home_units in self.later:
            if home_units is None:
                self.wait_units(sem, units)
            else:
                pl.when(self.at_home)(functools.partial(self.wait_units, sem, home_units))
                pl.when(jnp.logical_not(self.at_home))(functools.partial(self.wait_units, sem, units))


class Gather:
    def __init__(self, net, view, me, n, device, plan, pieces=None, partner=None, other=None):
        self.net, self.view, self.me, self.n, self.device = net, view, me, n, device
        self.pieces, self.partner, self.other = pieces, partner, other
        self.stages = PLANS[plan] if n == 8 else (tuple((0, None, o) for o in range(1, n)),)
        self.recv, self.halves = {}, {}
        if pieces is not None:
            self.recv[0], self.home_sem = net.take(), net.take()
            net.sent(self.home_sem, 2, 1)
        self.sem, units = net.take(), 0
        for stage in self.stages:
            for want, half, o in stage:
                relative = (want - o) % n
                if relative not in self.recv:
                    self.recv[relative] = net.take()
                units += 2 if half is None else 1
        net.sent(self.sem, units)
        self.here = set() if pieces is not None else {0}
        if partner is not None:
            self.cross_send, self.cross_recv = net.take(), net.take()
            net.sent(self.cross_send, 2 * n)

    def block(self, relative):
        return lax.rem(self.me + relative + 2 * self.n, self.n)

    def cross(self, relative):
        if self.partner is not None:
            got = self.view(self.block(relative), None)
            self.net.send(got, got, self.cross_send, self.cross_recv, self.partner)

    def arrive(self, relative):
        relative %= self.n
        if relative not in self.here:
            self.here.add(relative)
            self.net.wait(self.view(self.block(relative), None), self.recv[relative])
            return relative
        return None

    def start(self):
        if self.pieces is not None:
            self.pieces(0, self.home_sem, self.recv[0])
        self.stage(0)
        if self.pieces is None:
            self.cross(0)

    def stage(self, i):
        for want, half, o in self.stages[i]:
            if self.pieces is not None and want == 0:
                self.pieces(o, self.sem, self.recv[-o % self.n])
                continue
            new = self.arrive(want)
            got = self.view(self.block(want), half)
            self.net.send(got, got, self.sem, self.recv[(want - o) % self.n], self.device(o))
            if new is not None:
                self.cross(new)

    def finish(self):
        for relative in self.recv:
            new = self.arrive(relative)
            if new is not None:
                self.cross(new)

    def finish_cross(self):
        self.net.wait(self.other, self.cross_recv)


def interleave(*gathers):
    for i in range(1, max(len(g.stages) for g in gathers)):
        for g in gathers:
            if i < len(g.stages):
                g.stage(i)


def spread(pattern, rows):
    lane = lax.broadcasted_iota(jnp.int32, (rows // 2, 256), 1)
    halves = []
    for i in range(2):
        e = [pattern[i, j].astype(jnp.float32) for j in range(4)]
        low = jnp.where(lane < 64, e[0], e[1])
        high = jnp.where(lane < 192, e[2], e[3])
        halves.append(jnp.where(lane < 128, low, high))
    return jnp.concatenate(halves, axis=0)


def kernel(
    ny, nz, den_ref, cot_ref, pat_ref, fil_ref, pur_ref, grad_ref,
    am, aw, asq, ag, bm, bw, bg, keep_mine, keep_tile, part_s, part_g, wire_s, wire_g, got_s, got_g, square_end,
    total, end_p, end_g, got_p, got_d, sems,
):
    row, col = lax.axis_index("row"), lax.axis_index("col")
    x, y = lax.rem(row, X), lax.div(row, X)
    core, z = lax.rem(col, 2), lax.div(col, 2)
    slot, home = lax.rem(x, 2), lax.div(x, 2)

    def dev(yy, xx, zz, cc):
        return (yy * X + xx, zz * 2 + cc)

    def along_y(o, xx, cc):
        return dev(lax.rem(y + o + ny, ny), xx, z, cc)

    def along_z(o, xx, cc):
        return dev(y, xx, lax.rem(z + o + nz, nz), cc)

    def at_y(o):
        return along_y(o, x, core)

    def at_z(o):
        return along_z(o, x, core)

    partner = dev(y, x, z, 1 - core)
    others = [partner]
    for d in range(1, X):
        there = lax.rem(x + d, X)
        others += [dev(y, there, z, core), dev(y, there, z, 1 - core)]
    for n, along in ((ny, along_y), (nz, along_z)):
        for o in [o for a in range(1, FAR + 1) for o in (a, -a)] if n == 8 else range(1, n):
            others += [along(o, x, core), along(o, 2 * core, home), along(o, 2 * core + 1, home)]

    barrier = pltpu.get_barrier_semaphore()
    for other in others:
        pl.semaphore_signal(barrier, inc=1, device_id=other, device_id_type=MESH)
    keep_p = spread(pat_ref, 128)
    keep_f = spread(fil_ref, 128)
    bm[y, core] = (den_ref[...].astype(jnp.float32) * keep_p).astype(jnp.bfloat16)
    bw[y, core] = (-2.0 * cot_ref[...].astype(jnp.float32) * keep_f).astype(jnp.bfloat16)
    keep_mine[...] = keep_f.astype(jnp.bfloat16)
    pl.semaphore_wait(barrier, len(others))

    net = Net(sems, am, home == core)

    def swap_pieces(src, dst, along):
        def pieces(o, send, recv):
            for j in range(2):
                there = along(o, 2 * core + j, home)
                if o == 0:
                    is_self = jnp.logical_and(x == 2 * core + j, home == core)
                    net.send_or_keep(src(j), dst(slot), send, recv, there, is_self)
                else:
                    net.send(src(j), dst(slot), send, recv, there)

        return pieces

    def swap(src, dst):
        send, recv = net.take(), net.take()
        swap_pieces(src, dst, along_z)(0, send, recv)
        net.sent(send, 2, 1)
        return recv

    def to_rows(own, tile):
        return (lambda j: own.at[:, pl.ds(128 * j, 128)]), (lambda s: tile.at[pl.ds(pl.multiple_of(128 * s, 128), 128), :])

    def to_cols(tile, own):
        return (lambda j: tile.at[pl.ds(128 * j, 128), :]), (lambda s: own.at[:, pl.ds(pl.multiple_of(128 * s, 128), 128)])

    def rows_half(ref, half, size):
        return ref if half is None else ref.at[pl.ds(half * size, size), :]

    def b_gather(buf, plan, pieces=None):
        return Gather(
            net, lambda k, h: rows_half(buf.at[k, core], h, 64), y, ny, at_y, plan, pieces, partner, buf.at[:, 1 - core]
        )

    def a_gather(buf, plan, pieces=None):
        return Gather(net, lambda k, h: rows_half(buf.at[k], h, 128), z, nz, at_z, plan, pieces)

    def product(a, b, h):
        left = jnp.concatenate([a[k] for k in range(nz)], axis=1)
        right = b[:, h].reshape(ny * 128, 256)
        return jnp.dot(left, right, preferred_element_type=jnp.float32)

    def part(a, b, to, wire):
        for h in range(2):
            value = product(a, b, h)
            for i in range(2):
                to[2 * h + i] = value[:, 128 * i : 128 * i + 128]
                wire[2 * h + i] = value[:, 128 * i : 128 * i + 128].astype(MID_TYPE)

    def reduce_start(src, dst):
        send, recv = net.take(), net.take()
        for d in (2, 1, 3):
            there = lax.rem(x + d, X)
            net.send(src.at[there], dst.at[d], send, recv, dev(y, there, z, core))
        net.sent(send, 6 if MID_TYPE == jnp.bfloat16 else 12)
        return recv

    def reduce_end(src, dst, recv):
        net.wait(dst.at[pl.ds(1, X - 1)], recv)
        total = src[x]
        for d in range(1, X):
            total = total + dst[d].astype(jnp.float32)
        return total

    def end_start(src, dst):
        send, recv = net.take(), net.take()
        for j in range(2):
            for h in range(2):
                is_self = jnp.logical_and(x == 2 * core + j, core == h)
                net.send_or_keep(src.at[j, h], dst.at[x], send, recv, dev(y, 2 * core + j, z, h), is_self)
        scale = 1 if END_TYPE == jnp.bfloat16 else 2
        net.sent(send, 8 * scale, 6 * scale)
        return recv

    def end_sum(dst, recv):
        net.wait(dst, recv)
        value = dst[0].astype(jnp.float32)
        for s in range(1, X):
            value = value + dst[s].astype(jnp.float32)
        return value

    def split(value, h, to):
        for j in range(2):
            to[j, h] = value[128 * j : 128 * j + 128].astype(END_TYPE)

    w_src, w_dst = to_rows(bw.at[y, core], aw.at[z])
    m_src, m_dst = to_rows(bm.at[y, core], am.at[z])
    f_src, f_dst = to_rows(keep_mine, keep_tile)
    all_aw = a_gather(aw, PLAN["aw"], swap_pieces(w_src, w_dst, along_z))
    all_am = a_gather(am, PLAN["am"], swap_pieces(m_src, m_dst, along_z))
    all_bm = b_gather(bm, PLAN["bm"])
    all_aw.start()
    all_bm.start()
    all_am.start()
    f_recv = swap(f_src, f_dst)
    interleave(all_aw, all_bm, all_am)
    all_bm.finish()
    all_aw.finish()
    all_bm.finish_cross()

    part(aw, bm, part_g, wire_g)
    g_recv = reduce_start(wire_g, got_g)
    all_am.finish()
    part(am, bm, part_s, wire_s)
    s_recv = reduce_start(wire_s, got_s)
    all_bw = b_gather(bw, PLAN["bw"])
    all_bw.start()
    net.wait(keep_tile, f_recv)

    grad = -1.5 * aw[z].astype(jnp.float32) + reduce_end(part_g, got_g, g_recv)
    ag[z] = (grad * keep_tile[...].astype(jnp.float32)).astype(jnp.bfloat16)
    all_ag = a_gather(ag, PLAN["ag"])
    g_src = to_cols(ag.at[z], None)[0]
    g_dst = lambda s: bg.at[y, home, :, pl.ds(pl.multiple_of(128 * s, 128), 128)]
    g_pieces = swap_pieces(g_src, g_dst, along_y)
    all_bg = b_gather(bg, PLAN["bg"], g_pieces)
    all_bg.start()
    all_ag.start()

    asq[z] = (reduce_end(part_s, got_s, s_recv) * keep_tile[...].astype(jnp.float32)).astype(jnp.bfloat16)
    all_as = a_gather(asq, PLAN["asq"])
    all_as.start()
    q_src, q_dst = to_cols(asq.at[z], square_end)
    q_recv = swap(q_src, q_dst)
    interleave(all_bg, all_ag, all_as, all_bw)
    all_bw.finish()
    all_bg.finish()
    all_bw.finish_cross()
    all_as.finish()

    for h in range(2):
        split(product(asq, bm, h), h, end_p)
    p_recv = end_start(end_p, got_p)
    for h in range(2):
        total[h] = product(asq, bw, h)
    all_ag.finish()
    for h in range(2):
        total[h] += product(ag, bm, h)
    all_bg.finish_cross()
    for h in range(2):
        split(total[h] + product(am, bg, h), h, end_g)
    d_recv = end_start(end_g, got_d)

    net.wait(square_end, q_recv)
    cubic = end_sum(got_p, p_recv) * keep_mine[...].astype(jnp.float32)
    pur_ref[...] = (3.0 * square_end[...].astype(jnp.float32) - 2.0 * cubic).astype(jnp.bfloat16)
    grad_ref[...] = (end_sum(got_d, d_recv) * spread(pat_ref, 128)).astype(jnp.bfloat16)
    net.drain()


def on_device(ny, nz, density, cotangent, block_pattern, filter_pattern):
    bf16, f32 = jnp.bfloat16, jnp.float32
    left = pltpu.VMEM((nz, 256, 128), bf16)
    right = pltpu.VMEM((ny, 2, 128, 256), bf16)
    block = pltpu.VMEM((128, 256), bf16)
    vmem = pl.BlockSpec(memory_space=pltpu.VMEM)
    smem = pl.BlockSpec(memory_space=pltpu.SMEM)
    return pl.pallas_call(
        functools.partial(kernel, ny, nz),
        out_shape=(jax.ShapeDtypeStruct((128, 256), bf16),) * 2,
        in_specs=[vmem, vmem, smem, smem],
        out_specs=(vmem, vmem),
        scratch_shapes=[left] * 4
        + [right] * 3
        + [
            block,
            pltpu.VMEM((256, 128), bf16),
            pltpu.VMEM((X, 256, 128), f32),
            pltpu.VMEM((X, 256, 128), f32),
            pltpu.VMEM((X, 256, 128), MID_TYPE),
            pltpu.VMEM((X, 256, 128), MID_TYPE),
            pltpu.VMEM((X, 256, 128), MID_TYPE),
            pltpu.VMEM((X, 256, 128), MID_TYPE),
            block,
            pltpu.VMEM((2, 256, 256), f32),
            pltpu.VMEM((2, 2, 128, 256), END_TYPE),
            pltpu.VMEM((2, 2, 128, 256), END_TYPE),
            pltpu.VMEM((X, 128, 256), END_TYPE),
            pltpu.VMEM((X, 128, 256), END_TYPE),
            pltpu.SemaphoreType.DMA((N_SEM,)),
        ],
        compiler_params=pltpu.CompilerParams(collective_id=0, has_side_effects=True),
    )(density, cotangent, block_pattern, filter_pattern)


def solution(mesh):
    ny, nz = mesh.shape["row"] // X, mesh.shape["col"] // 2
    placed = (P("row", "col"),) * 4
    return jax.shard_map(
        functools.partial(on_device, ny, nz),
        mesh=mesh,
        in_specs=placed,
        out_specs=(P("row", "col"), P("row", "col")),
        check_vma=False,
    )
```

time: 80.2 us -> 64.9 us (0.81)
  Pallas kernels: 77.2 us -> 61.9 us
    pallas_call x1, Pallas kernels: 77.2 us -> 61.9 us  [on_device(): pl.pallas_call(functools.partial(kernel, ny, nz), out_shape=(jax.ShapeDty...]
where the time goes in v2:
time: 64.9 us; the launch traced here: 64.6 us
  Pallas kernels  61.9 us (95%)
  local copies, waits for them, and re-layouts  2.14 us (3%)
  between operations  0.65 us (1%)
    pallas_call x1, Pallas kernels, on_device(): pl.pallas_call(functools.partial(kernel, ny, nz), out_shape=(jax.ShapeDty...  61.9 us
    unnamed x4, local copies, waits for them, and re-layouts  2.14 us

profile of v2, /device:TPU:1, one launch (start us, length us, event | category | flops | bytes accessed | tf_op | source)
XLA Modules:
  0.0 64.6 jit_solution(2102053928717472241)
XLA Ops:
  0.6 61.9 %shard_map.59 = (bf16[128,256]{1,0:T(8,128)(2,1)}, bf16[128,256]{1,0:T(8,128)(2,1)}) custom-call(bf16[128,256]{1,0:T(8,128)(2,1)} %den_ref.1, bf16[128,256]{1,0:T(8,128)(2,1)} %cot_ref.1, s32[2,4]{1,0:T(2,128)} %pat_ref.1, s32[2,4]{1,0:T(2,128)} %fil_ref.1), custom_call_target="tpu_custom_call" | custom-call | tf_op jit(solution)/shard_map/pallas_call | solution.py:358
  62.5 0.0 copy-start
  62.5 1.5 %copy.8 = bf16[128,256]{1,0:T(8,128)(2,1)} copy(bf16[128,256]{1,0:T(8,128)(2,1)} %get-tuple-element.4) | data formatting | bytes 131072
  64.0 0.0 copy-done
  64.0 0.6 copy.9
Async XLA Ops:
  62.5 1.5 %copy-start = (bf16[128,256]{1,0:T(8,128)(2,1)S(1)}, bf16[128,256]{1,0:T(8,128)(2,1)}, u32[]{:S(2)}) copy-start(bf16[128,256]{1,0:T(8,128)(2,1)} %get-tuple-element.5) | copy-start | bytes 196612

commit v3 on v2

--- a/solution.py
+++ b/solution.py
@@ -11,13 +11,13 @@
 X = 4
 MID_TYPE = jnp.bfloat16
 END_TYPE = jnp.bfloat16
-N_SEM = 100
-PLAN = dict(bm="two", aw="two", am="two", bw="two", ag="two", asq="two", bg="two")
+N_SEM = 80
+PLAN = dict(bm="two", aw="far", am="far", bw="two", ag="two", asq="two", bg="far")
 PLANS = {
-    "ring": (((0, None, 1), (0, None, -1)), ((-1, None, 1), (1, None, -1)), ((-2, None, 1), (2, None, -1)), ((-3, 0, 1), (3, 1, -1))),
-    "two": (((0, None, 2), (0, None, -2), (0, None, 1), (0, None, -1)), ((-2, None, 1), (2, None, -1), (-2, 0, 2), (2, 1, -2))),
+    "two": (((0, None, 2), (0, None, -2), (0, None, 1), (0, None, -1)), ((-2, 0, 2), (2, 1, -2), (-2, None, 1), (2, None, -1))),
+    "far": (((0, None, 2), (0, None, -2)), ((0, None, 1), (0, None, -1), (-2, 0, 2), (2, 1, -2), (-2, None, 1), (2, None, -1))),
 }
-FAR = 2
+OFFSETS = (1, -1, 2, -2)
 
 
 class Net:
@@ -117,7 +117,7 @@
 
     def stage(self, i):
         for want, half, o in self.stages[i]:
-            if self.pieces is not None and want == 0:
+            if self.pieces is not None and want == 0 and i == 0:
                 self.pieces(o, self.sem, self.recv[-o % self.n])
                 continue
             new = self.arrive(want)
@@ -155,7 +155,7 @@
 
 
 def kernel(
-    ny, nz, den_ref, cot_ref, pat_ref, fil_ref, pur_ref, grad_ref,
+    ny, nz, den_hbm, cot_hbm, pat_hbm, fil_hbm, pur_ref, grad_ref, den_ref, cot_ref, pat_ref, fil_ref,
     am, aw, asq, ag, bm, bw, bg, keep_mine, keep_tile, part_s, part_g, wire_s, wire_g, got_s, got_g, square_end,
     total, end_p, end_g, got_p, got_d, sems,
 ):
@@ -185,12 +185,20 @@
         there = lax.rem(x + d, X)
         others += [dev(y, there, z, core), dev(y, there, z, 1 - core)]
     for n, along in ((ny, along_y), (nz, along_z)):
-        for o in [o for a in range(1, FAR + 1) for o in (a, -a)] if n == 8 else range(1, n):
-            others += [along(o, x, core), along(o, 2 * core, home), along(o, 2 * core + 1, home)]
+        for o in OFFSETS if n == 8 else range(1, n):
+            others += [along(o, x, core)]
+            if abs(o) == 2 or n != 8:
+                others += [along(o, 2 * core, home), along(o, 2 * core + 1, home)]
 
     barrier = pltpu.get_barrier_semaphore()
     for other in others:
         pl.semaphore_signal(barrier, inc=1, device_id=other, device_id_type=MESH)
+    loads = ((den_hbm, den_ref), (cot_hbm, cot_ref), (pat_hbm, pat_ref), (fil_hbm, fil_ref))
+    loads = [pltpu.make_async_copy(src, dst, sems.at[N_SEM + i]) for i, (src, dst) in enumerate(loads)]
+    for load in loads:
+        load.start()
+    for load in loads:
+        load.wait()
     keep_p = spread(pat_ref, 128)
     keep_f = spread(fil_ref, 128)
     bm[y, core] = (den_ref[...].astype(jnp.float32) * keep_p).astype(jnp.bfloat16)
@@ -286,14 +294,15 @@
     w_src, w_dst = to_rows(bw.at[y, core], aw.at[z])
     m_src, m_dst = to_rows(bm.at[y, core], am.at[z])
     f_src, f_dst = to_rows(keep_mine, keep_tile)
+    all_bm = b_gather(bm, PLAN["bm"])
+    all_bw = b_gather(bw, PLAN["bw"])
     all_aw = a_gather(aw, PLAN["aw"], swap_pieces(w_src, w_dst, along_z))
     all_am = a_gather(am, PLAN["am"], swap_pieces(m_src, m_dst, along_z))
-    all_bm = b_gather(bm, PLAN["bm"])
     all_aw.start()
     all_bm.start()
     all_am.start()
     f_recv = swap(f_src, f_dst)
-    interleave(all_aw, all_bm, all_am)
+    interleave(all_bm, all_aw, all_am)
     all_bm.finish()
     all_aw.finish()
     all_bm.finish_cross()
@@ -303,7 +312,6 @@
     all_am.finish()
     part(am, bm, part_s, wire_s)
     s_recv = reduce_start(wire_s, got_s)
-    all_bw = b_gather(bw, PLAN["bw"])
     all_bw.start()
     net.wait(keep_tile, f_recv)
 
@@ -322,11 +330,10 @@
     all_as.start()
     q_src, q_dst = to_cols(asq.at[z], square_end)
     q_recv = swap(q_src, q_dst)
-    interleave(all_bg, all_ag, all_as, all_bw)
+    interleave(all_ag, all_bg, all_as, all_bw)
     all_bw.finish()
-    all_bg.finish()
+    all_as.finish()
     all_bw.finish_cross()
-    all_as.finish()
 
     for h in range(2):
         split(product(asq, bm, h), h, end_p)
@@ -336,9 +343,10 @@
     all_ag.finish()
     for h in range(2):
         total[h] += product(ag, bm, h)
+    all_bg.finish()
+    split(total[core] + product(am, bg, core), core, end_g)
     all_bg.finish_cross()
-    for h in range(2):
-        split(total[h] + product(am, bg, h), h, end_g)
+    split(total[1 - core] + product(am, bg, 1 - core), 1 - core, end_g)
     d_recv = end_start(end_g, got_d)
 
     net.wait(square_end, q_recv)
@@ -354,13 +362,14 @@
     right = pltpu.VMEM((ny, 2, 128, 256), bf16)
     block = pltpu.VMEM((128, 256), bf16)
     vmem = pl.BlockSpec(memory_space=pltpu.VMEM)
-    smem = pl.BlockSpec(memory_space=pltpu.SMEM)
     return pl.pallas_call(
         functools.partial(kernel, ny, nz),
         out_shape=(jax.ShapeDtypeStruct((128, 256), bf16),) * 2,
-        in_specs=[vmem, vmem, smem, smem],
+        in_specs=[pl.BlockSpec(memory_space=pl.ANY)] * 4,
         out_specs=(vmem, vmem),
-        scratch_shapes=[left] * 4
+        scratch_shapes=[block] * 2
+        + [pltpu.SMEM((2, 4), jnp.int32)] * 2
+        + [left] * 4
         + [right] * 3
         + [
             block,
@@ -377,7 +386,7 @@
             pltpu.VMEM((2, 2, 128, 256), END_TYPE),
             pltpu.VMEM((X, 128, 256), END_TYPE),
             pltpu.VMEM((X, 128, 256), END_TYPE),
-            pltpu.SemaphoreType.DMA((N_SEM,)),
+            pltpu.SemaphoreType.DMA((N_SEM + 4,)),
         ],
         compiler_params=pltpu.CompilerParams(collective_id=0, has_side_effects=True),
     )(density, cotangent, block_pattern, filter_pattern)

time: 64.9 us -> 63.1 us (0.972)
  Pallas kernels: 61.9 us -> 60.1 us
    pallas_call x1, Pallas kernels: 61.9 us -> 60.1 us  [on_device(): pl.pallas_call(functools.partial(kernel, ny, nz), out_shape=(jax.ShapeDty...]
where the time goes in v3:
time: 63.1 us; the launch traced here: 62.9 us
  Pallas kernels  60.1 us (95%)
  local copies, waits for them, and re-layouts  2.14 us (3%)
  between operations  0.65 us (1%)
    pallas_call x1, Pallas kernels, on_device(): pl.pallas_call(functools.partial(kernel, ny, nz), out_shape=(jax.ShapeDty...  60.1 us
    unnamed x4, local copies, waits for them, and re-layouts  2.14 us

profile of v3, /device:TPU:1, one launch (start us, length us, event | category | flops | bytes accessed | tf_op | source)
XLA Modules:
  0.0 62.9 jit_solution(9010715822423732981)
XLA Ops:
  0.6 60.1 %shard_map.59 = (bf16[128,256]{1,0:T(8,128)(2,1)}, bf16[128,256]{1,0:T(8,128)(2,1)}) custom-call(bf16[128,256]{1,0:T(8,128)(2,1)} %den_hbm.1, bf16[128,256]{1,0:T(8,128)(2,1)} %cot_hbm.1, s32[2,4]{1,0:T(2,128)} %pat_hbm.1, s32[2,4]{1,0:T(2,128)} %fil_hbm.1), custom_call_target="tpu_custom_call" | custom-call | tf_op jit(solution)/shard_map/pallas_call | solution.py:365
  60.8 0.0 copy-start
  60.8 1.5 %copy.8 = bf16[128,256]{1,0:T(8,128)(2,1)} copy(bf16[128,256]{1,0:T(8,128)(2,1)} %get-tuple-element.4) | data formatting | bytes 131072
  62.3 0.0 copy-done
  62.3 0.6 %copy.9 = bf16[128,256]{1,0:T(8,128)(2,1)} copy(bf16[128,256]{1,0:T(8,128)(2,1)S(1)} %copy-done) | data formatting | bytes 131072
Async XLA Ops:
  60.8 1.5 %copy-start = (bf16[128,256]{1,0:T(8,128)(2,1)S(1)}, bf16[128,256]{1,0:T(8,128)(2,1)}, u32[]{:S(2)}) copy-start(bf16[128,256]{1,0:T(8,128)(2,1)} %get-tuple-element.5) | copy-start | bytes 196612

commit v4 on v3

--- a/solution.py
+++ b/solution.py
@@ -328,9 +328,10 @@
     asq[z] = (reduce_end(part_s, got_s, s_recv) * keep_tile[...].astype(jnp.float32)).astype(jnp.bfloat16)
     all_as = a_gather(asq, PLAN["asq"])
     all_as.start()
+    interleave(all_bw)
     q_src, q_dst = to_cols(asq.at[z], square_end)
     q_recv = swap(q_src, q_dst)
-    interleave(all_ag, all_bg, all_as, all_bw)
+    interleave(all_ag, all_bg, all_as)
     all_bw.finish()
     all_as.finish()
     all_bw.finish_cross()

time: 63.1 us -> 62.8 us (level)
  no operation moved by 1% of the time
where the time goes in v4:
time: 62.8 us; the launch traced here: 62.6 us
  Pallas kernels  59.8 us (95%)
  local copies, waits for them, and re-layouts  2.14 us (3%)
  between operations  0.65 us (1%)
    pallas_call x1, Pallas kernels, on_device(): pl.pallas_call(functools.partial(kernel, ny, nz), out_shape=(jax.ShapeDty...  59.8 us
    unnamed x4, local copies, waits for them, and re-layouts  2.14 us

profile of v4, /device:TPU:1, one launch (start us, length us, event | category | flops | bytes accessed | tf_op | source)
XLA Modules:
  0.0 62.6 jit_solution(10709489215648371940)
XLA Ops:
  0.6 59.8 %shard_map.59 = (bf16[128,256]{1,0:T(8,128)(2,1)}, bf16[128,256]{1,0:T(8,128)(2,1)}) custom-call(bf16[128,256]{1,0:T(8,128)(2,1)} %den_hbm.1, bf16[128,256]{1,0:T(8,128)(2,1)} %cot_hbm.1, s32[2,4]{1,0:T(2,128)} %pat_hbm.1, s32[2,4]{1,0:T(2,128)} %fil_hbm.1), custom_call_target="tpu_custom_call" | custom-call | tf_op jit(solution)/shard_map/pallas_call | solution.py:366
  60.4 0.0 copy-start
  60.4 1.5 %copy.8 = bf16[128,256]{1,0:T(8,128)(2,1)} copy(bf16[128,256]{1,0:T(8,128)(2,1)} %get-tuple-element.4) | data formatting | bytes 131072
  61.9 0.0 copy-done
  62.0 0.6 %copy.9 = bf16[128,256]{1,0:T(8,128)(2,1)} copy(bf16[128,256]{1,0:T(8,128)(2,1)S(1)} %copy-done) | data formatting | bytes 131072
Async XLA Ops:
  60.4 1.5 %copy-start = (bf16[128,256]{1,0:T(8,128)(2,1)S(1)}, bf16[128,256]{1,0:T(8,128)(2,1)}, u32[]{:S(2)}) copy-start(bf16[128,256]{1,0:T(8,128)(2,1)} %get-tuple-element.5) | copy-start | bytes 196612
